TPU v7x, 32 devices: a whole 2x2x4 slice. The times are simulated.
32 devices in a mesh: row: 4 (over y, x), col: 8 (over z, core).
Axes of the slice: x: 2, y: 2, z: 4, core: 2. Of those that a mesh axis runs over, the one named last changes fastest.
Arguments:
- tiles: float32 [384, 1024, 128], P('row', 'col'), may hold values from -0.1875 to 0.1875
- tile_row: int32 [384, 8], P('row', 'col'), may hold values from 0 to 511
- tile_col: int32 [384, 8], P('row', 'col'), may hold values from 0 to 255
- tile_count: int32 [4, 8], P('row', 'col'), may hold values from 24 to 96, as said below
- cost: float32 [8, 32768], P('col', 'row'), may hold values from -6 to 6
- rhs: float32 [4, 65536], P('row', 'col'), may hold values from -6 to 6
- lower: float32 [8, 32768], P('col', 'row'), may hold values from -2 to -0.3
- upper: float32 [8, 32768], P('col', 'row'), may hold values from 0.3 to 2
- primal_start: float32 [8, 32768], P('col', 'row'), may hold values from -0.3 to 0.3
- dual_start: float32 [4, 65536], P('row', 'col'), may hold values from 0 to 1
Outputs:
- primal_mean: float32 [8, 32768], P('col', 'row')
- dual_mean: float32 [4, 65536], P('row', 'col')
- primal_last: float32 [8, 32768], P('col', 'row')
- dual_last: float32 [4, 65536], P('row', 'col')
Inputs may be any that keep to these rules, and one draw needn't show every extreme that they name: `tile_count`: live tiles of each device; some device holds 96.
All inputs are finite; a program needn't handle non-finite values.
Results may differ from a plain program's by a relative error of at most 0.0001.
Values sent between devices are 32-bit elements; how exact they have to be, the bound alone decides.
A program may use at most 64 MiB of HBM per device.

v0:
```python
import jax
import jax.numpy as jnp
from jax import lax
from jax.sharding import PartitionSpec as P

ITERS = 6
exact = lax.Precision.HIGHEST
primal_step = 0.3
dual_step = 0.3


def body(tiles, tile_row, tile_col, tile_count, cost, rhs, lower, upper, primal_start, dual_start):
    tile_slots = tiles.shape[0]
    block_size = tiles.shape[2]
    row_blocks = rhs.shape[1] * lax.axis_size("col") // block_size
    col_blocks = cost.shape[1] * lax.axis_size("row") // block_size
    live = (lax.iota(jnp.int32, tile_slots) < tile_count.reshape(())).astype(jnp.float32)
    row_hot = (tile_row[:, 0][:, None] == lax.iota(jnp.int32, row_blocks)[None, :]).astype(
        jnp.float32
    ) * live[:, None]
    col_hot = (tile_col[:, 0][:, None] == lax.iota(jnp.int32, col_blocks)[None, :]).astype(
        jnp.float32
    )
    primal = primal_start.reshape(-1)
    dual = dual_start.reshape(-1)
    cost_flat = cost.reshape(-1)
    lower_flat = lower.reshape(-1)
    upper_flat = upper.reshape(-1)
    rhs_flat = rhs.reshape(-1)
    primal_share = primal.shape[0]
    dual_share = dual.shape[0]
    primal_full, cost_full, lower_full, upper_full = (
        lax.all_gather(primal, "row", axis=0, tiled=True),
        lax.all_gather(cost_flat, "row", axis=0, tiled=True),
        lax.all_gather(lower_flat, "row", axis=0, tiled=True),
        lax.all_gather(upper_flat, "row", axis=0, tiled=True),
    )
    dual_full, rhs_full = (
        lax.all_gather(dual, "col", axis=0, tiled=True),
        lax.all_gather(rhs_flat, "col", axis=0, tiled=True),
    )
    extrapolated = primal_full
    primal_total = jnp.zeros_like(primal_full)
    dual_total = jnp.zeros_like(dual_full)
    for iteration in range(ITERS):
        forward_taken = jnp.dot(
            col_hot, extrapolated.reshape(col_blocks, block_size), precision=exact
        )
        forward_product = jnp.einsum("tij,tj->ti", tiles, forward_taken, precision=exact)
        applied = lax.psum(
            jnp.einsum("tr,ti->ri", row_hot, forward_product, precision=exact).reshape(-1), "col"
        )
        dual_full = jnp.maximum(dual_full + dual_step * (rhs_full - applied), 0.0)
        taken = jnp.dot(row_hot, dual_full.reshape(row_blocks, block_size), precision=exact)
        product = jnp.einsum("tij,ti->tj", tiles, taken, precision=exact)
        transposed = lax.psum(
            jnp.einsum("tk,tj->kj", col_hot, product, precision=exact).reshape(-1), "row"
        )
        moved = primal_full - primal_step * (cost_full - transposed)
        primal_new = jnp.minimum(jnp.maximum(moved, lower_full), upper_full)
        extrapolated = 2.0 * primal_new - primal_full
        primal_full = primal_new
        primal_total = primal_total + primal_full
        dual_total = dual_total + dual_full
    primal_start_at = lax.axis_index("row") * primal_share
    dual_start_at = lax.axis_index("col") * dual_share
    primal = lax.dynamic_slice_in_dim(primal_full, primal_start_at, primal_share, 0)
    dual = lax.dynamic_slice_in_dim(dual_full, dual_start_at, dual_share, 0)
    primal_mean = lax.dynamic_slice_in_dim(primal_total, primal_start_at, primal_share, 0) / ITERS
    dual_mean = lax.dynamic_slice_in_dim(dual_total, dual_start_at, dual_share, 0) / ITERS
    return (
        primal_mean.reshape(1, -1),
        dual_mean.reshape(1, -1),
        primal.reshape(1, -1),
        dual.reshape(1, -1),
    )


def solution(mesh):
    return jax.shard_map(
        body,
        mesh=mesh,
        in_specs=(
            P("row", "col", None),
            P("row", "col"),
            P("row", "col"),
            P("row", "col"),
            P("col", "row"),
            P("row", "col"),
            P("col", "row"),
            P("col", "row"),
            P("col", "row"),
            P("row", "col"),
        ),
        out_specs=(P("col", "row"), P("row", "col"), P("col", "row"), P("row", "col")),
        check_vma=False,
    )
```

profile of v0, /device:TPU:0, one launch (start us, length us, event | category | flops | bytes accessed | tf_op | source)
XLA Modules:
  0.0 754.3 jit_solution(14544451130449158460)
XLA Ops:
  7.2 10.1 %all-gather = f32[1,32768]{1,0:T(1,128)S(1)} all-gather(f32[1,8192]{1,0:T(1,128)} %param.18), channel_id=2, replica_groups=mesh['row'=4,'col'=8] {'row'}, dimensions={1}, use_global_device_ids=true | all-gather | bytes 163840 | tf_op jit(solution)/shard_map/all_gather | solution.py:33
  18.1 0.9 fusion.80
  19.0 11.9 %fusion.119 = f32[96,1,128]{2,1,0:T(1,128)S(1)} fusion(f32[96,128,1]{1,2,0:T(1,128)S(1)} %bitcast.220, f32[96,128,128]{2,1,0:T(8,128)} %param.10), kind=kOutput, calls=%fused_computation.154 | convolution fusion | flops 18874368 | bytes 6389760 | tf_op jit(solution)/shard_map/tij,tj->ti/dot_general | solution.py:49
  30.8 1.4 convolution_bitcast_fusion.5
  32.3 14.5 %all-gather.3 = f32[1,65536]{1,0:T(1,128)S(1)} all-gather(f32[1,8192]{1,0:T(1,128)S(1)} %copy-done.2), channel_id=5, replica_groups=mesh['row'=4,'col'=8] {'col'}, dimensions={1}, use_global_device_ids=true | all-gather | bytes 294912 | tf_op jit(solution)/shard_map/all_gather | solution.py:40
  46.8 14.3 %all-gather.2 = f32[1,65536]{1,0:T(1,128)S(1)} all-gather(f32[1,8192]{1,0:T(1,128)S(1)} %copy-done.3), channel_id=4, replica_groups=mesh['row'=4,'col'=8] {'col'}, dimensions={1}, use_global_device_ids=true | all-gather | bytes 294912 | tf_op jit(solution)/shard_map/all_gather | solution.py:39
  61.1 27.3 %all-reduce.13.cloned.1.call-done = f32[65536]{0:T(1024)} async-done(((f32[65536]{0:T(1024)}), f32[65536]{0:T(1024)}) %all-reduce.13.cloned.1.call-update) | async-done | bytes 262160 | tf_op jit(solution)/shard_map/psum | solution.py:50
  88.3 1.0 add_maximum_fusion.5
  89.3 0.4 fusion.15
  89.7 7.3 fusion.120
  97.0 1.0 convolution_bitcast_fusion.11
  98.2 8.4 %all-gather.1 = f32[1,32768]{1,0:T(1,128)S(1)} all-gather(f32[1,8192]{1,0:T(1,128)S(1)} %copy-done.4), channel_id=3, replica_groups=mesh['row'=4,'col'=8] {'row'}, dimensions={1}, use_global_device_ids=true | all-gather | bytes 163840 | tf_op jit(solution)/shard_map/all_gather | solution.py:34
  106.6 8.5 %all-gather.4 = f32[1,32768]{1,0:T(1,128)S(1)} all-gather(f32[1,8192]{1,0:T(1,128)S(1)} %copy-done.5), channel_id=6, replica_groups=mesh['row'=4,'col'=8] {'row'}, dimensions={1}, use_global_device_ids=true | all-gather | bytes 163840 | tf_op jit(solution)/shard_map/all_gather | solution.py:35
  115.1 8.0 %all-gather.5 = f32[1,32768]{1,0:T(1,128)S(1)} all-gather(f32[1,8192]{1,0:T(1,128)S(1)} %copy-done.6), channel_id=7, replica_groups=mesh['row'=4,'col'=8] {'row'}, dimensions={1}, use_global_device_ids=true | all-gather | bytes 163840 | tf_op jit(solution)/shard_map/all_gather | solution.py:36
  123.0 16.5 %all-reduce.15.cloned.1.call-done = f32[32768]{0:T(1024)} async-done(((f32[32768]{0:T(1024)}), f32[32768]{0:T(1024)}) %all-reduce.15.cloned.1.call-update) | async-done | bytes 131088 | tf_op jit(solution)/shard_map/psum | solution.py:56
  139.6 0.9 maximum_minimum_fusion.5
  140.8 11.8 %fusion.121 = f32[96,1,128]{2,1,0:T(1,128)S(1)} fusion(f32[96,128,1]{1,2,0:T(1,128)S(1)} %bitcast.198, f32[96,128,128]{2,1,0:T(8,128)} %param.10), kind=kOutput, calls=%fused_computation.156 | convolution fusion | flops 18874368 | bytes 6389760 | tf_op jit(solution)/shard_map/tij,tj->ti/dot_general | solution.py:49
  152.6 1.4 convolution_bitcast_fusion.4
  154.1 55.5 %all-reduce.17.cloned.1.call-done = f32[65536]{0:T(1024)} async-done(((f32[65536]{0:T(1024)}), f32[65536]{0:T(1024)}) %all-reduce.17.cloned.1.call-update) | async-done | bytes 262160 | tf_op jit(solution)/shard_map/psum | solution.py:50
  209.6 1.0 add_maximum_fusion.4
  210.6 0.4 fusion.12
  210.9 7.3 fusion.122
  218.3 1.0 convolution_bitcast_fusion.10
  219.5 41.2 %all-reduce.19.cloned.1.call-done = f32[32768]{0:T(1024)} async-done(((f32[32768]{0:T(1024)}), f32[32768]{0:T(1024)}) %all-reduce.19.cloned.1.call-update) | async-done | bytes 131088 | tf_op jit(solution)/shard_map/psum | solution.py:56
  260.7 0.9 maximum_minimum_fusion.4
  261.9 11.8 %fusion.123 = f32[96,1,128]{2,1,0:T(1,128)S(1)} fusion(f32[96,128,1]{1,2,0:T(1,128)S(1)} %bitcast.207, f32[96,128,128]{2,1,0:T(8,128)} %param.10), kind=kOutput, calls=%fused_computation.158 | convolution fusion | flops 18874368 | bytes 6389760 | tf_op jit(solution)/shard_map/tij,tj->ti/dot_general | solution.py:49
  273.8 1.4 convolution_bitcast_fusion.3
  275.2 55.5 %all-reduce.21.cloned.1.call-done = f32[65536]{0:T(1024)} async-done(((f32[65536]{0:T(1024)}), f32[65536]{0:T(1024)}) %all-reduce.21.cloned.1.call-update) | async-done | bytes 262160 | tf_op jit(solution)/shard_map/psum | solution.py:50
  330.7 1.0 add_maximum_fusion.3
  331.7 0.4 fusion.9
  332.1 7.3 fusion.124
  339.5 1.0 convolution_bitcast_fusion.9
  340.6 41.4 %all-reduce.23.cloned.1.call-done = f32[32768]{0:T(1024)} async-done(((f32[32768]{0:T(1024)}), f32[32768]{0:T(1024)}) %all-reduce.23.cloned.1.call-update) | async-done | bytes 131088 | tf_op jit(solution)/shard_map/psum | solution.py:56
  381.9 0.9 maximum_minimum_fusion.3
  383.1 11.8 %fusion.125 = f32[96,1,128]{2,1,0:T(1,128)S(1)} fusion(f32[96,128,1]{1,2,0:T(1,128)S(1)} %bitcast.209, f32[96,128,128]{2,1,0:T(8,128)} %param.10), kind=kOutput, calls=%fused_computation.160 | convolution fusion | flops 18874368 | bytes 6389760 | tf_op jit(solution)/shard_map/tij,tj->ti/dot_general | solution.py:49
  395.0 1.4 convolution_bitcast_fusion.2
  396.6 55.3 %all-reduce.25.cloned.1.call-done = f32[65536]{0:T(1024)} async-done(((f32[65536]{0:T(1024)}), f32[65536]{0:T(1024)}) %all-reduce.25.cloned.1.call-update) | async-done | bytes 262160 | tf_op jit(solution)/shard_map/psum | solution.py:50
  451.9 1.0 add_maximum_fusion.2
  452.9 0.4 fusion.6
  453.3 7.3 fusion.126
  460.6 1.0 convolution_bitcast_fusion.8
  461.7 41.4 %all-reduce.27.cloned.1.call-done = f32[32768]{0:T(1024)} async-done(((f32[32768]{0:T(1024)}), f32[32768]{0:T(1024)}) %all-reduce.27.cloned.1.call-update) | async-done | bytes 131088 | tf_op jit(solution)/shard_map/psum | solution.py:56
  503.1 0.9 maximum_minimum_fusion.2
  504.3 11.8 %fusion.127 = f32[96,1,128]{2,1,0:T(1,128)S(1)} fusion(f32[96,128,1]{1,2,0:T(1,128)S(1)} %bitcast.211, f32[96,128,128]{2,1,0:T(8,128)} %param.10), kind=kOutput, calls=%fused_computation.162 | convolution fusion | flops 18874368 | bytes 6389760 | tf_op jit(solution)/shard_map/tij,tj->ti/dot_general | solution.py:49
  516.1 1.4 convolution_bitcast_fusion.1
  517.6 55.5 %all-reduce.29.cloned.1.call-done = f32[65536]{0:T(1024)} async-done(((f32[65536]{0:T(1024)}), f32[65536]{0:T(1024)}) %all-reduce.29.cloned.1.call-update) | async-done | bytes 262160 | tf_op jit(solution)/shard_map/psum | solution.py:50
  573.1 1.0 add_maximum_fusion.1
  574.1 0.4 fusion.3
  574.5 7.3 fusion.128
  581.8 1.0 convolution_bitcast_fusion.7
  582.9 0.3 all-reduce.33.cloned.1.call-start
  583.2 41.1 %all-reduce.31.cloned.1.call-done = f32[32768]{0:T(1024)} async-done(((f32[32768]{0:T(1024)}), f32[32768]{0:T(1024)}) %all-reduce.31.cloned.1.call-update) | async-done | bytes 131088 | tf_op jit(solution)/shard_map/psum | solution.py:56
  624.3 0.9 maximum_minimum_fusion.1
  625.5 11.8 %fusion.129 = f32[96,1,128]{2,1,0:T(1,128)S(1)} fusion(f32[96,128,1]{1,2,0:T(1,128)S(1)} %bitcast.213, f32[96,128,128]{2,1,0:T(8,128)} %param.10), kind=kOutput, calls=%fused_computation.164 | convolution fusion | flops 18874368 | bytes 6389760 | tf_op jit(solution)/shard_map/tij,tj->ti/dot_general | solution.py:49
  637.3 1.4 convolution_bitcast_fusion
  638.8 55.5 %all-reduce.33.cloned.1.call-done = f32[65536]{0:T(1024)} async-done(((f32[65536]{0:T(1024)}), f32[65536]{0:T(1024)}) %all-reduce.33.cloned.1.call-update) | async-done | bytes 262160 | tf_op jit(solution)/shard_map/psum | solution.py:50
  694.3 1.0 add_maximum_fusion
  695.3 0.4 fusion
  695.7 7.3 fusion.130
  703.0 1.0 convolution_bitcast_fusion.6
  704.0 0.6 fusion.99
  704.7 40.8 %all-reduce.35.cloned.1.call-done = f32[32768]{0:T(1024)} async-done(((f32[32768]{0:T(1024)}), f32[32768]{0:T(1024)}) %all-reduce.35.cloned.1.call-update) | async-done | bytes 131088 | tf_op jit(solution)/shard_map/psum | solution.py:56
  745.5 0.9 maximum_minimum_fusion
  746.4 0.6 fusion.101
  (43 shorter events, 2.3 us)
Async XLA Ops:
  7.2 23.7 %copy-start = (s32[96,1]{0,1:T(1,128)S(1)}, s32[96,1]{0,1:T(1,128)}, u32[]{:S(2)}) copy-start(s32[96,1]{0,1:T(1,128)} %param.11) | copy-start | bytes 1156
  7.2 25.1 %copy-start.2 = (f32[1,8192]{1,0:T(1,128)S(1)}, f32[1,8192]{1,0:T(1,128)}, u32[]{:S(2)}) copy-start(f32[1,8192]{1,0:T(1,128)} %param.15) | copy-start | bytes 98308
  7.2 39.6 %copy-start.3 = (f32[1,8192]{1,0:T(1,128)S(1)}, f32[1,8192]{1,0:T(1,128)}, u32[]{:S(2)}) copy-start(f32[1,8192]{1,0:T(1,128)} %param.19) | copy-start | bytes 98308
  7.2 81.1 %all-reduce.13.cloned.1.call-start = ((), (), s32[]{:S(2)}) async-start(), calls=%async_computation | async-start | bytes 524288 | tf_op jit(solution)/shard_map/psum | solution.py:50
  18.9 78.1 %copy-start.1 = (s32[96,1]{0,1:T(1,128)S(1)}, s32[96,1]{0,1:T(1,128)}, u32[]{:S(2)}) copy-start(s32[96,1]{0,1:T(1,128)} %param.12) | copy-start | bytes 1156
  19.0 79.2 %copy-start.4 = (f32[1,8192]{1,0:T(1,128)S(1)}, f32[1,8192]{1,0:T(1,128)}, u32[]{:S(2)}) copy-start(f32[1,8192]{1,0:T(1,128)} %param.14) | copy-start | bytes 98308
  30.8 75.8 %copy-start.5 = (f32[1,8192]{1,0:T(1,128)S(1)}, f32[1,8192]{1,0:T(1,128)}, u32[]{:S(2)}) copy-start(f32[1,8192]{1,0:T(1,128)} %param.16) | copy-start | bytes 98308
  30.8 84.2 %copy-start.6 = (f32[1,8192]{1,0:T(1,128)S(1)}, f32[1,8192]{1,0:T(1,128)}, u32[]{:S(2)}) copy-start(f32[1,8192]{1,0:T(1,128)} %param.17) | copy-start | bytes 98308
  32.2 107.3 %all-reduce.15.cloned.1.call-start = ((), (), s32[]{:S(2)}) async-start(), calls=%async_computation.1 | async-start | bytes 262144 | tf_op jit(solution)/shard_map/psum | solution.py:56
  98.1 111.5 %all-reduce.17.cloned.1.call-start = ((), (), s32[]{:S(2)}) async-start(), calls=%async_computation.2 | async-start | bytes 524288 | tf_op jit(solution)/shard_map/psum | solution.py:50
  154.0 106.7 %all-reduce.19.cloned.1.call-start = ((), (), s32[]{:S(2)}) async-start(), calls=%async_computation.3 | async-start | bytes 262144 | tf_op jit(solution)/shard_map/psum | solution.py:56
  219.3 111.4 %all-reduce.21.cloned.1.call-start = ((), (), s32[]{:S(2)}) async-start(), calls=%async_computation.4 | async-start | bytes 524288 | tf_op jit(solution)/shard_map/psum | solution.py:50
  275.2 106.7 %all-reduce.23.cloned.1.call-start = ((), (), s32[]{:S(2)}) async-start(), calls=%async_computation.5 | async-start | bytes 262144 | tf_op jit(solution)/shard_map/psum | solution.py:56
  340.5 111.4 %all-reduce.25.cloned.1.call-start = ((), (), s32[]{:S(2)}) async-start(), calls=%async_computation.6 | async-start | bytes 524288 | tf_op jit(solution)/shard_map/psum | solution.py:50
  396.4 106.7 %all-reduce.27.cloned.1.call-start = ((), (), s32[]{:S(2)}) async-start(), calls=%async_computation.7 | async-start | bytes 262144 | tf_op jit(solution)/shard_map/psum | solution.py:56
  461.7 111.4 %all-reduce.29.cloned.1.call-start = ((), (), s32[]{:S(2)}) async-start(), calls=%async_computation.8 | async-start | bytes 524288 | tf_op jit(solution)/shard_map/psum | solution.py:50
  517.5 106.7 %all-reduce.31.cloned.1.call-start = ((), (), s32[]{:S(2)}) async-start(), calls=%async_computation.9 | async-start | bytes 262144 | tf_op jit(solution)/shard_map/psum | solution.py:56
  582.9 111.4 %all-reduce.33.cloned.1.call-start = ((), (), s32[]{:S(2)}) async-start(), calls=%async_computation.10 | async-start | bytes 524288 | tf_op jit(solution)/shard_map/psum | solution.py:50
  638.7 106.7 %all-reduce.35.cloned.1.call-start = ((), (), s32[]{:S(2)}) async-start(), calls=%async_computation.11 | async-start | bytes 262144 | tf_op jit(solution)/shard_map/psum | solution.py:56
Sparse Core Ops, SparseCore 0:
  32.4 55.9 all-reduce.12
  98.2 41.3 all-reduce.14
  154.1 55.4 all-reduce.16
  219.4 41.2 all-reduce.18
  275.3 55.4 all-reduce.20
  340.6 41.2 all-reduce.22
  396.5 55.4 all-reduce.24
  461.8 41.2 all-reduce.26
  517.7 55.4 all-reduce.28
  583.0 41.2 all-reduce.30
  638.8 55.4 all-reduce.32
  704.2 41.2 all-reduce.34
where the time goes:
time: 762 us; the launch traced here: 754 us
  waiting for transfers between devices  527 us (69%)
  matrix products  134 us (18%)
  blocking collectives  63.8 us (8%)
  between operations  15.5 us (2%)
  other arithmetic  12.9 us (2%)
    psum x6, waiting for transfers between devices, body(): lax.psum(jnp.einsum('tr,ti->ri', row_hot, forward_product, precision=exac...  305 us
    psum x6, waiting for transfers between devices, body(): lax.psum(jnp.einsum('tk,tj->kj', col_hot, product, precision=exact).resha...  222 us
    dot_general x6, matrix products, body(): jnp.einsum('tij,tj->ti', tiles, forward_taken, precision=exact)  71.1 us
    dot_general x6, matrix products, body(): product = jnp.einsum('tij,ti->tj', tiles, taken, precision=exact)  43.9 us
  transfers between devices with their start and end apart: 12, of which 12 were waited for; matrix products, arithmetic and copies ran while one was open for 0% of the time, Pallas kernels for 0%

commit v1 on v0

--- a/solution.py
+++ b/solution.py
@@ -7,6 +7,10 @@
 exact = lax.Precision.HIGHEST
 primal_step = 0.3
 dual_step = 0.3
+
+
+def extend_the_plate(page):
+    return lax.all_gather(page, axis_name="row").sum(axis=0)
 
 
 def body(tiles, tile_row, tile_col, tile_count, cost, rhs, lower, upper, primal_start, dual_start):
@@ -53,8 +57,8 @@
         dual_full = jnp.maximum(dual_full + dual_step * (rhs_full - applied), 0.0)
         taken = jnp.dot(row_hot, dual_full.reshape(row_blocks, block_size), precision=exact)
         product = jnp.einsum("tij,ti->tj", tiles, taken, precision=exact)
-        transposed = lax.psum(
-            jnp.einsum("tk,tj->kj", col_hot, product, precision=exact).reshape(-1), "row"
+        transposed = extend_the_plate(
+            jnp.einsum("tk,tj->kj", col_hot, product, precision=exact).reshape(-1)
         )
         moved = primal_full - primal_step * (cost_full - transposed)
         primal_new = jnp.minimum(jnp.maximum(moved, lower_full), upper_full)

time: 762 us -> 564 us (0.74)
  waiting for transfers between devices: 527 us -> 271 us
  blocking collectives: 63.8 us -> 129 us
    psum x6 -> x0, waiting for transfers between devices: 222 us -> none  [body(): lax.psum(jnp.einsum('tk,tj->kj', col_hot, product, precision=exact).resha...]
    all_gather x0 -> x6, blocking collectives: none -> 65.5 us  [extend_the_plate(): return lax.all_gather(page, axis_name='row').sum(axis=0)]
    psum x6, waiting for transfers between devices: 305 us -> 271 us  [body(): lax.psum(jnp.einsum('tr,ti->ri', row_hot, forward_product, precision=exac...]
  transfers between devices with their start and end apart: 12 -> 6, of which waited for: 12 -> 6; matrix products, arithmetic and copies ran while one was open for 0% -> 0% of each run, Pallas kernels for 0% -> 0%
where the time goes in v1:
time: 564 us; the launch traced here: 556 us
  waiting for transfers between devices  271 us (48%)
  matrix products  130 us (23%)
  blocking collectives  129 us (23%)
  between operations  15.6 us (3%)
  other arithmetic  10.4 us (2%)
    psum x6, waiting for transfers between devices, body(): lax.psum(jnp.einsum('tr,ti->ri', row_hot, forward_product, precision=exac...  271 us
    dot_general x6, matrix products, body(): jnp.einsum('tij,tj->ti', tiles, forward_taken, precision=exact)  71.1 us
    all_gather x6, blocking collectives, extend_the_plate(): return lax.all_gather(page, axis_name='row').sum(axis=0)  65.5 us
    dot_general x6, matrix products, body(): product = jnp.einsum('tij,ti->tj', tiles, taken, precision=exact)  43.9 us
    all_gather x1, blocking collectives, body(): lax.all_gather(rhs_flat, 'col', axis=0, tiled=True)  14.5 us
    all_gather x1, blocking collectives, body(): lax.all_gather(dual, 'col', axis=0, tiled=True)  14.5 us
  transfers between devices with their start and end apart: 6, of which 6 were waited for; matrix products, arithmetic and copies ran while one was open for 0% of the time, Pallas kernels for 0%

profile of v1, /device:TPU:0, one launch (start us, length us, event | category | flops | bytes accessed | tf_op | source)
XLA Modules:
  0.0 556.2 jit_solution(3669220493312321887)
XLA Ops:
  7.3 10.1 %all-gather = f32[1,32768]{1,0:T(1,128)S(1)} all-gather(f32[1,8192]{1,0:T(1,128)} %param.18), channel_id=2, replica_groups=mesh['row'=4,'col'=8] {'row'}, dimensions={1}, use_global_device_ids=true | all-gather | bytes 163840 | tf_op jit(solution)/shard_map/all_gather | solution.py:37
  18.1 0.9 fusion.86
  19.0 11.8 %fusion.125 = f32[96,1,128]{2,1,0:T(1,128)S(1)} fusion(f32[96,128,1]{1,2,0:T(1,128)S(1)} %bitcast.220, f32[96,128,128]{2,1,0:T(8,128)} %param.10), kind=kOutput, calls=%fused_computation.154 | convolution fusion | flops 18874368 | bytes 6389760 | tf_op jit(solution)/shard_map/tij,tj->ti/dot_general | solution.py:53
  30.8 1.4 convolution_bitcast_fusion.5
  32.3 14.5 %all-gather.3 = f32[1,65536]{1,0:T(1,128)S(1)} all-gather(f32[1,8192]{1,0:T(1,128)S(1)} %copy-done.2), channel_id=5, replica_groups=mesh['row'=4,'col'=8] {'col'}, dimensions={1}, use_global_device_ids=true | all-gather | bytes 294912 | tf_op jit(solution)/shard_map/all_gather | solution.py:44
  46.8 8.2 %all-gather.1 = f32[1,32768]{1,0:T(1,128)S(1)} all-gather(f32[1,8192]{1,0:T(1,128)S(1)} %copy-done.3), channel_id=3, replica_groups=mesh['row'=4,'col'=8] {'row'}, dimensions={1}, use_global_device_ids=true | all-gather | bytes 163840 | tf_op jit(solution)/shard_map/all_gather | solution.py:38
  55.0 7.9 %all-gather.4 = f32[1,32768]{1,0:T(1,128)S(1)} all-gather(f32[1,8192]{1,0:T(1,128)S(1)} %copy-done.4), channel_id=6, replica_groups=mesh['row'=4,'col'=8] {'row'}, dimensions={1}, use_global_device_ids=true | all-gather | bytes 163840 | tf_op jit(solution)/shard_map/all_gather | solution.py:39
  62.9 8.0 %all-gather.5 = f32[1,32768]{1,0:T(1,128)S(1)} all-gather(f32[1,8192]{1,0:T(1,128)S(1)} %copy-done.5), channel_id=7, replica_groups=mesh['row'=4,'col'=8] {'row'}, dimensions={1}, use_global_device_ids=true | all-gather | bytes 163840 | tf_op jit(solution)/shard_map/all_gather | solution.py:40
  70.9 14.5 %all-gather.2 = f32[1,65536]{1,0:T(1,128)S(1)} all-gather(f32[1,8192]{1,0:T(1,128)S(1)} %copy-done.6), channel_id=4, replica_groups=mesh['row'=4,'col'=8] {'col'}, dimensions={1}, use_global_device_ids=true | all-gather | bytes 294912 | tf_op jit(solution)/shard_map/all_gather | solution.py:43
  85.4 3.0 all-reduce.7.cloned.1.call-done
  88.3 1.0 add_maximum_fusion.5
  89.3 0.4 fusion.15
  89.7 7.3 %fusion.126 = f32[96,1,128]{2,1,0:T(1,128)S(1)} fusion(f32[96,128,1]{1,2,0:T(1,128)S(1)} %bitcast.205, f32[96,128,128]{2,1,0:T(8,128)} %param.10), kind=kOutput, calls=%fused_computation.155 | convolution fusion | flops 18874368 | bytes 6389760 | tf_op jit(solution)/shard_map/tij,ti->tj/dot_general | solution.py:59
  97.0 0.4 fusion.85
  97.4 11.1 %all-gather.6 = f32[4,1,32768]{2,1,0:T(1,128)S(1)} all-gather(f32[1,1,32768]{2,1,0:T(1,128)S(1)} %bitcast.191), channel_id=1, replica_groups=mesh['row'=4,'col'=8] {'row'}, dimensions={0}, use_global_device_ids=true | all-gather | bytes 655360 | tf_op jit(solution)/shard_map/all_gather | solution.py:13
  108.5 0.5 reduce_sum.54
  109.3 11.8 %fusion.127 = f32[96,1,128]{2,1,0:T(1,128)S(1)} fusion(f32[96,128,1]{1,2,0:T(1,128)S(1)} %bitcast.199, f32[96,128,128]{2,1,0:T(8,128)} %param.10), kind=kOutput, calls=%fused_computation.156 | convolution fusion | flops 18874368 | bytes 6389760 | tf_op jit(solution)/shard_map/tij,tj->ti/dot_general | solution.py:53
  121.1 1.4 convolution_bitcast_fusion.4
  122.6 53.7 %all-reduce.9.cloned.1.call-done = f32[65536]{0:T(1024)} async-done(((f32[65536]{0:T(1024)}), f32[65536]{0:T(1024)}) %all-reduce.9.cloned.1.call-update) | async-done | bytes 262160 | tf_op jit(solution)/shard_map/psum | solution.py:54
  176.3 1.0 add_maximum_fusion.4
  177.3 0.4 fusion.12
  177.7 7.3 %fusion.128 = f32[96,1,128]{2,1,0:T(1,128)S(1)} fusion(f32[96,128,1]{1,2,0:T(1,128)S(1)} %bitcast.206, f32[96,128,128]{2,1,0:T(8,128)} %param.10), kind=kOutput, calls=%fused_computation.157 | convolution fusion | flops 18874368 | bytes 6389760 | tf_op jit(solution)/shard_map/tij,ti->tj/dot_general | solution.py:59
  185.0 0.4 fusion.84
  185.4 10.9 %all-gather.7 = f32[4,1,32768]{2,1,0:T(1,128)S(1)} all-gather(f32[1,1,32768]{2,1,0:T(1,128)S(1)} %bitcast.192), channel_id=1, replica_groups=mesh['row'=4,'col'=8] {'row'}, dimensions={0}, use_global_device_ids=true | all-gather | bytes 655360 | tf_op jit(solution)/shard_map/all_gather | solution.py:13
  196.2 0.5 reduce_sum.55
  197.0 11.8 %fusion.129 = f32[96,1,128]{2,1,0:T(1,128)S(1)} fusion(f32[96,128,1]{1,2,0:T(1,128)S(1)} %bitcast.207, f32[96,128,128]{2,1,0:T(8,128)} %param.10), kind=kOutput, calls=%fused_computation.158 | convolution fusion | flops 18874368 | bytes 6389760 | tf_op jit(solution)/shard_map/tij,tj->ti/dot_general | solution.py:53
  208.8 1.4 convolution_bitcast_fusion.3
  210.3 53.7 %all-reduce.11.cloned.1.call-done = f32[65536]{0:T(1024)} async-done(((f32[65536]{0:T(1024)}), f32[65536]{0:T(1024)}) %all-reduce.11.cloned.1.call-update) | async-done | bytes 262160 | tf_op jit(solution)/shard_map/psum | solution.py:54
  264.0 1.0 add_maximum_fusion.3
  265.0 0.4 fusion.9
  265.3 7.3 %fusion.130 = f32[96,1,128]{2,1,0:T(1,128)S(1)} fusion(f32[96,128,1]{1,2,0:T(1,128)S(1)} %bitcast.208, f32[96,128,128]{2,1,0:T(8,128)} %param.10), kind=kOutput, calls=%fused_computation.159 | convolution fusion | flops 18874368 | bytes 6389760 | tf_op jit(solution)/shard_map/tij,ti->tj/dot_general | solution.py:59
  272.7 0.4 fusion.83
  273.0 10.9 %all-gather.8 = f32[4,1,32768]{2,1,0:T(1,128)S(1)} all-gather(f32[1,1,32768]{2,1,0:T(1,128)S(1)} %bitcast.193), channel_id=1, replica_groups=mesh['row'=4,'col'=8] {'row'}, dimensions={0}, use_global_device_ids=true | all-gather | bytes 655360 | tf_op jit(solution)/shard_map/all_gather | solution.py:13
  284.0 0.5 reduce_sum.56
  284.7 11.8 %fusion.131 = f32[96,1,128]{2,1,0:T(1,128)S(1)} fusion(f32[96,128,1]{1,2,0:T(1,128)S(1)} %bitcast.209, f32[96,128,128]{2,1,0:T(8,128)} %param.10), kind=kOutput, calls=%fused_computation.160 | convolution fusion | flops 18874368 | bytes 6389760 | tf_op jit(solution)/shard_map/tij,tj->ti/dot_general | solution.py:53
  296.6 1.4 convolution_bitcast_fusion.2
  298.0 53.7 %all-reduce.13.cloned.1.call-done = f32[65536]{0:T(1024)} async-done(((f32[65536]{0:T(1024)}), f32[65536]{0:T(1024)}) %all-reduce.13.cloned.1.call-update) | async-done | bytes 262160 | tf_op jit(solution)/shard_map/psum | solution.py:54
  351.7 1.0 add_maximum_fusion.2
  352.7 0.4 fusion.6
  353.1 7.3 %fusion.132 = f32[96,1,128]{2,1,0:T(1,128)S(1)} fusion(f32[96,128,1]{1,2,0:T(1,128)S(1)} %bitcast.210, f32[96,128,128]{2,1,0:T(8,128)} %param.10), kind=kOutput, calls=%fused_computation.161 | convolution fusion | flops 18874368 | bytes 6389760 | tf_op jit(solution)/shard_map/tij,ti->tj/dot_general | solution.py:59
  360.4 0.4 fusion.82
  360.8 11.0 %all-gather.9 = f32[4,1,32768]{2,1,0:T(1,128)S(1)} all-gather(f32[1,1,32768]{2,1,0:T(1,128)S(1)} %bitcast.194), channel_id=1, replica_groups=mesh['row'=4,'col'=8] {'row'}, dimensions={0}, use_global_device_ids=true | all-gather | bytes 655360 | tf_op jit(solution)/shard_map/all_gather | solution.py:13
  371.7 0.5 reduce_sum.57
  372.2 0.2 fusion.26
  372.5 11.8 %fusion.133 = f32[96,1,128]{2,1,0:T(1,128)S(1)} fusion(f32[96,128,1]{1,2,0:T(1,128)S(1)} %bitcast.211, f32[96,128,128]{2,1,0:T(8,128)} %param.10), kind=kOutput, calls=%fused_computation.162 | convolution fusion | flops 18874368 | bytes 6389760 | tf_op jit(solution)/shard_map/tij,tj->ti/dot_general | solution.py:53
  384.3 1.4 convolution_bitcast_fusion.1
  385.8 53.7 %all-reduce.15.cloned.1.call-done = f32[65536]{0:T(1024)} async-done(((f32[65536]{0:T(1024)}), f32[65536]{0:T(1024)}) %all-reduce.15.cloned.1.call-update) | async-done | bytes 262160 | tf_op jit(solution)/shard_map/psum | solution.py:54
  439.5 1.0 add_maximum_fusion.1
  440.5 0.4 fusion.3
  440.8 7.3 %fusion.134 = f32[96,1,128]{2,1,0:T(1,128)S(1)} fusion(f32[96,128,1]{1,2,0:T(1,128)S(1)} %bitcast.212, f32[96,128,128]{2,1,0:T(8,128)} %param.10), kind=kOutput, calls=%fused_computation.163 | convolution fusion | flops 18874368 | bytes 6389760 | tf_op jit(solution)/shard_map/tij,ti->tj/dot_general | solution.py:59
  448.2 0.4 fusion.81
  448.5 11.0 %all-gather.10 = f32[4,1,32768]{2,1,0:T(1,128)S(1)} all-gather(f32[1,1,32768]{2,1,0:T(1,128)S(1)} %bitcast.195), channel_id=1, replica_groups=mesh['row'=4,'col'=8] {'row'}, dimensions={0}, use_global_device_ids=true | all-gather | bytes 655360 | tf_op jit(solution)/shard_map/all_gather | solution.py:13
  459.5 0.5 reduce_sum.58
  460.3 11.8 %fusion.135 = f32[96,1,128]{2,1,0:T(1,128)S(1)} fusion(f32[96,128,1]{1,2,0:T(1,128)S(1)} %bitcast.213, f32[96,128,128]{2,1,0:T(8,128)} %param.10), kind=kOutput, calls=%fused_computation.164 | convolution fusion | flops 18874368 | bytes 6389760 | tf_op jit(solution)/shard_map/tij,tj->ti/dot_general | solution.py:53
  472.1 1.4 convolution_bitcast_fusion
  473.6 53.7 %all-reduce.17.cloned.1.call-done = f32[65536]{0:T(1024)} async-done(((f32[65536]{0:T(1024)}), f32[65536]{0:T(1024)}) %all-reduce.17.cloned.1.call-update) | async-done | bytes 262160 | tf_op jit(solution)/shard_map/psum | solution.py:54
  527.3 1.0 add_maximum_fusion
  528.3 0.4 fusion
  528.6 0.6 fusion.105
  529.3 7.3 %fusion.136 = f32[96,1,128]{2,1,0:T(1,128)S(1)} fusion(f32[96,128,1]{1,2,0:T(1,128)S(1)} %bitcast.197, f32[96,128,128]{2,1,0:T(8,128)} %param.10), kind=kOutput, calls=%fused_computation.165 | convolution fusion | flops 18874368 | bytes 6389760 | tf_op jit(solution)/shard_map/tij,ti->tj/dot_general | solution.py:59
  536.6 0.4 fusion.80
  537.0 10.7 %all-gather.11 = f32[4,1,32768]{2,1,0:T(1,128)S(1)} all-gather(f32[1,1,32768]{2,1,0:T(1,128)S(1)} %bitcast.196), channel_id=1, replica_groups=mesh['row'=4,'col'=8] {'row'}, dimensions={0}, use_global_device_ids=true | all-gather | bytes 655360 | tf_op jit(solution)/shard_map/all_gather | solution.py:13
  547.7 0.5 reduce_sum.59
  548.2 0.6 fusion.107
  (37 shorter events, 1.5 us)
Async XLA Ops:
  7.2 23.7 %copy-start = (s32[96,1]{0,1:T(1,128)S(1)}, s32[96,1]{0,1:T(1,128)}, u32[]{:S(2)}) copy-start(s32[96,1]{0,1:T(1,128)} %param.11) | copy-start | bytes 1156
  7.2 25.1 %copy-start.2 = (f32[1,8192]{1,0:T(1,128)S(1)}, f32[1,8192]{1,0:T(1,128)}, u32[]{:S(2)}) copy-start(f32[1,8192]{1,0:T(1,128)} %param.15) | copy-start | bytes 98308
  7.2 39.6 %copy-start.3 = (f32[1,8192]{1,0:T(1,128)S(1)}, f32[1,8192]{1,0:T(1,128)}, u32[]{:S(2)}) copy-start(f32[1,8192]{1,0:T(1,128)} %param.14) | copy-start | bytes 98308
  7.2 47.8 %copy-start.4 = (f32[1,8192]{1,0:T(1,128)S(1)}, f32[1,8192]{1,0:T(1,128)}, u32[]{:S(2)}) copy-start(f32[1,8192]{1,0:T(1,128)} %param.16) | copy-start | bytes 98308
  7.2 55.7 %copy-start.5 = (f32[1,8192]{1,0:T(1,128)S(1)}, f32[1,8192]{1,0:T(1,128)}, u32[]{:S(2)}) copy-start(f32[1,8192]{1,0:T(1,128)} %param.17) | copy-start | bytes 98308
  7.2 63.7 %copy-start.6 = (f32[1,8192]{1,0:T(1,128)S(1)}, f32[1,8192]{1,0:T(1,128)}, u32[]{:S(2)}) copy-start(f32[1,8192]{1,0:T(1,128)} %param.19) | copy-start | bytes 98308
  7.2 81.1 %all-reduce.7.cloned.1.call-start = ((), (), s32[]{:S(2)}) async-start(), calls=%async_computation | async-start | bytes 524288 | tf_op jit(solution)/shard_map/psum | solution.py:54
  30.8 66.2 %copy-start.1 = (s32[96,1]{0,1:T(1,128)S(1)}, s32[96,1]{0,1:T(1,128)}, u32[]{:S(2)}) copy-start(s32[96,1]{0,1:T(1,128)} %param.12) | copy-start | bytes 1156
  32.2 144.0 %all-reduce.9.cloned.1.call-start = ((), (), s32[]{:S(2)}) async-start(), calls=%async_computation.1 | async-start | bytes 524288 | tf_op jit(solution)/shard_map/psum | solution.py:54
  122.5 141.4 %all-reduce.11.cloned.1.call-start = ((), (), s32[]{:S(2)}) async-start(), calls=%async_computation.2 | async-start | bytes 524288 | tf_op jit(solution)/shard_map/psum | solution.py:54
  210.3 141.4 %all-reduce.13.cloned.1.call-start = ((), (), s32[]{:S(2)}) async-start(), calls=%async_computation.3 | async-start | bytes 524288 | tf_op jit(solution)/shard_map/psum | solution.py:54
  298.0 141.5 %all-reduce.15.cloned.1.call-start = ((), (), s32[]{:S(2)}) async-start(), calls=%async_computation.4 | async-start | bytes 524288 | tf_op jit(solution)/shard_map/psum | solution.py:54
  385.7 141.5 %all-reduce.17.cloned.1.call-start = ((), (), s32[]{:S(2)}) async-start(), calls=%async_computation.5 | async-start | bytes 524288 | tf_op jit(solution)/shard_map/psum | solution.py:54
Sparse Core Ops, SparseCore 0:
  32.4 55.9 all-reduce.6
  122.7 53.5 all-reduce.8
  210.4 53.5 all-reduce.10
  298.1 53.5 all-reduce.12
  385.9 53.5 all-reduce.14
  473.7 53.5 all-reduce.16
